TPU v7x, 32 devices: a whole 2x2x4 slice. The times are simulated.
32 devices in a mesh: row: 4 (over y, core), blk: 8 (over z, x).
Axes of the slice: x: 2, y: 2, z: 4, core: 2. Of those that a mesh axis runs over, the one named last changes fastest.
Arguments:
- right_side: float32 [4, 8, 8, 32, 256], P('row', 'blk')
- noise_level: float32 [4, 8, 8, 256], P('row', 'blk'), may hold values from 3 to 6
- near_blocks: bfloat16 [4, 8, 8, 9, 256, 256], P('row', 'blk'), as said below
- skeleton_basis: bfloat16 [4, 8, 8, 64, 256], P('row', 'blk'), may hold values from -0.125 to 0.125
- skeleton_index: int32 [4, 8, 64], P('row', 'blk'), may hold values from 0 to 2047, as said below
- far_list: int32 [4, 8, 7], P('row', 'blk'), may hold values from 0 to 7, as said below
- couplings: bfloat16 [4, 8, 7, 64, 64], P('row', 'blk'), as said below
Outputs:
- solution: float32 [4, 8, 8, 32, 256], P('row', 'blk')
- residual: float32 [4, 8, 8, 32, 256], P('row', 'blk')
- quadratic: float32 [32], replicated
Inputs may be any that keep to these rules, and one draw needn't show every extreme that they name: `far_list`: each device's 7 entries are distinct, none is the device's own blk index, and the two cyclic neighbours along blk are always among them; box b lists box b' exactly when b' lists b, and within a row every box's far boxes lie at the same set of cyclic offsets from its own index. `couplings`: the coupling that box b holds for far box b' is the transpose of the one that b' holds for b. `near_blocks`: A leaf's block for near slot s is the transpose of the block that its slot-s neighbour holds for slot 8 - s; slot 4 blocks are symmetric. `skeleton_index`: each device's 64 entries are distinct tracers of its 2048.
All inputs are finite; a program needn't handle non-finite values.
Results may differ from a plain program's by a relative error of at most 0.03.
Values may be sent and summed in bfloat16 or wider, within the bound.
A program may use at most 64 MiB of HBM per device.

v0:
```python
import jax
import jax.numpy as jnp
from jax import lax
from jax.sharding import PartitionSpec as P

ITERS = 4
LEAF_ROWS = 2
LEAF_COLS = 4


def extended_2(array, sides, width):
    for axis, dim in sides:
        count, length = (lax.axis_size(axis), array.shape[dim])
        up = [(i, (i + 1) % count) for i in range(count)]
        down = [(j, i) for i, j in up]
        last = lax.slice_in_dim(array, length - width, length, axis=dim)
        leading = lax.slice_in_dim(array, 0, width, axis=dim)
        before = lax.ppermute(last, axis, up)
        after = lax.ppermute(leading, axis, down)
        array = jnp.concatenate([before, array, after], axis=dim)
    return array


def local(
    right_side, noise_level, near_blocks, skeleton_basis, skeleton_index, far_list, couplings
):
    local_noise = noise_level[0, 0][:, None, :]
    leaf_count = near_blocks.shape[2]
    width = near_blocks.shape[4]
    blocks_grid = near_blocks[0, 0].reshape(LEAF_ROWS, LEAF_COLS, 9, width, width)
    basis_local = skeleton_basis[0, 0]
    skeleton_local = skeleton_index[0, 0]
    far_local = far_list[0, 0]
    coupling_local = couplings[0, 0]
    points = basis_local.shape[2]
    owner_leaf = skeleton_local // points
    owner_point = skeleton_local % points

    def column_sum(values):
        return jnp.sum(values, axis=(0, 1, 2, 4))

    def residual_sum(values):
        return lax.psum(column_sum(values * values), ("row", "blk"))

    solution = jnp.zeros_like(right_side)
    residual = right_side
    direction = right_side
    norm_now = residual_sum(residual)
    for step_index in range(ITERS):
        rounded = direction.astype(jnp.bfloat16)
        own_field = rounded[0, 0]
        columns = own_field.shape[1]
        leaf_grid = own_field.reshape(LEAF_ROWS, LEAF_COLS, columns, width)
        extended = extended_2(leaf_grid, (("row", 0), ("blk", 1)), 1)
        sources = jnp.stack(
            [
                extended[slot // 3 : slot // 3 + LEAF_ROWS, slot % 3 : slot % 3 + LEAF_COLS]
                for slot in range(9)
            ],
            axis=2,
        )
        near = jnp.einsum(
            "abkci,abkij->abcj", sources, blocks_grid, preferred_element_type=jnp.float32
        )
        result = near.reshape(leaf_count, columns, width)
        picked = own_field[owner_leaf, :, owner_point].astype(jnp.float32)
        skeleton = picked.T + jnp.einsum(
            "lci,lki->ck", own_field, basis_local, preferred_element_type=jnp.float32
        )
        all_skeletons = lax.all_gather(
            skeleton.astype(jnp.bfloat16)[None], "blk", axis=0, tiled=True
        )
        selected = all_skeletons[far_local]
        far_sum = jnp.einsum(
            "jck,jkm->cm", selected, coupling_local, preferred_element_type=jnp.float32
        )
        result = result + jnp.einsum(
            "ck,lki->lci",
            far_sum.astype(jnp.bfloat16),
            basis_local,
            preferred_element_type=jnp.float32,
        )
        result = result.at[owner_leaf, :, owner_point].add(far_sum.T)
        applied = (local_noise * direction[0, 0] + result)[None, None]
        curve = lax.psum(column_sum(direction * applied), ("row", "blk"))
        step_size = norm_now / curve
        solution = solution + step_size[:, None] * direction
        residual = residual - step_size[:, None] * applied
        norm_next = residual_sum(residual)
        direction = residual + (norm_next / norm_now)[:, None] * direction
        norm_now = norm_next
    total = lax.psum(column_sum(right_side * solution), ("row", "blk"))
    tracer_count = (
        lax.axis_size("row") * lax.axis_size("blk") * right_side.shape[2] * right_side.shape[4]
    )
    quadratic = total / tracer_count
    return (solution, residual, quadratic)


def solution(mesh):
    return jax.shard_map(
        local,
        mesh=mesh,
        in_specs=(
            P("row", "blk", None, None, None),
            P("row", "blk", None, None),
            P("row", "blk", None, None, None, None),
            P("row", "blk", None, None, None),
            P("row", "blk", None),
            P("row", "blk", None),
            P("row", "blk", None, None, None),
        ),
        out_specs=(P("row", "blk", None, None, None), P("row", "blk", None, None, None), P()),
        check_vma=False,
    )
```

profile of v0, /device:TPU:0, one launch (start us, length us, event | category | flops | bytes accessed | tf_op | source)
XLA Modules:
  0.0 537.6 jit_solution(16591721626279821936)
XLA Ops:
  5.8 30.8 %all-gather = bf16[256,64]{1,0:T(8,128)(2,1)S(1)} all-gather(bf16[32,64]{1,0:T(8,128)(2,1)S(1)} %fusion.12), channel_id=2, replica_groups=mesh['row'=4,'blk'=8] {'blk'}, dimensions={0}, use_global_device_ids=true | all-gather | bytes 36864 | tf_op jit(solution)/shard_map/all_gather | solution.py:70
  37.3 4.2 collective-permute-start.3
  43.5 5.1 collective-permute-done.2
  48.8 5.4 %fusion.95 = f32[2,4,32,256,1]{3,2,4,1,0:T(8,128)S(1)} fusion(bf16[2,4,9,32,256]{4,3,2,1,0:T(8,128)(2,1)S(1)} %fusion.58, bf16[2,4,9,256,256]{4,3,2,1,0:T(8,128)(2,1)} %bitcast.461), kind=kOutput, calls=%fused_computation.214 | convolution fusion | flops 301989888 | bytes 10878976 | tf_op jit(solution)/shard_map/abkci,abkij->abcj/dot_general | solution.py:62
  54.7 3.7 scatter_fusion
  59.0 36.9 %all-reduce = (f32[32]{0:T(128)S(1)}, f32[32]{0:T(128)S(1)}) all-reduce(f32[32]{0:T(128)S(1)} %get-tuple-element.32, f32[32]{0:T(128)S(1)} %fusion.16), channel_id=1, replica_groups=mesh['row'=4,'blk'=8] {'row','blk'}, use_global_device_ids=true, to_apply=%region_1.2 | all-reduce | flops 64 | bytes 512 | tf_op jit(solution)/shard_map/psum | solution.py:43
  96.1 42.0 %psum.65 = f32[32]{0:T(128)S(1)} all-reduce(f32[32]{0:T(128)S(1)} %multiply_reduce_fusion.3), channel_id=1, replica_groups=mesh['row'=4,'blk'=8] {'row','blk'}, use_global_device_ids=true, to_apply=%region_6.7 | all-reduce | flops 32 | bytes 256 | tf_op jit(solution)/shard_map/psum | solution.py:43
  140.2 30.6 %all-gather.1 = bf16[256,64]{1,0:T(8,128)(2,1)S(1)} all-gather(bf16[32,64]{1,0:T(8,128)(2,1)S(1)} %fusion.13), channel_id=3, replica_groups=mesh['row'=4,'blk'=8] {'blk'}, dimensions={0}, use_global_device_ids=true | all-gather | bytes 36864 | tf_op jit(solution)/shard_map/all_gather | solution.py:70
  176.5 5.1 collective-permute-done.6
  181.8 5.4 %fusion.96 = f32[2,4,32,256,1]{3,2,4,1,0:T(8,128)S(1)} fusion(bf16[2,4,9,32,256]{4,3,2,1,0:T(8,128)(2,1)S(1)} %fusion.48, bf16[2,4,9,256,256]{4,3,2,1,0:T(8,128)(2,1)} %bitcast.462), kind=kOutput, calls=%fused_computation.215 | convolution fusion | flops 301989888 | bytes 10878976 | tf_op jit(solution)/shard_map/abkci,abkij->abcj/dot_general | solution.py:62
  191.8 36.9 %psum.66 = f32[32]{0:T(128)S(1)} all-reduce(f32[32]{0:T(128)S(1)} %fusion.19), channel_id=1, replica_groups=mesh['row'=4,'blk'=8] {'row','blk'}, use_global_device_ids=true, to_apply=%region_9.10 | all-reduce | flops 32 | bytes 256 | tf_op jit(solution)/shard_map/psum | solution.py:85
  229.0 41.7 %psum.67 = f32[32]{0:T(128)S(1)} all-reduce(f32[32]{0:T(128)S(1)} %get-tuple-element.13), channel_id=1, replica_groups=mesh['row'=4,'blk'=8] {'row','blk'}, use_global_device_ids=true, to_apply=%region_11.12 | all-reduce | flops 32 | bytes 256 | tf_op jit(solution)/shard_map/psum | solution.py:43
  272.9 30.5 %all-gather.2 = bf16[256,64]{1,0:T(8,128)(2,1)S(1)} all-gather(bf16[32,64]{1,0:T(8,128)(2,1)S(1)} %fusion.14), channel_id=4, replica_groups=mesh['row'=4,'blk'=8] {'blk'}, dimensions={0}, use_global_device_ids=true | all-gather | bytes 36864 | tf_op jit(solution)/shard_map/all_gather | solution.py:70
  309.2 5.1 collective-permute-done.10
  314.5 5.4 %fusion.97 = f32[2,4,32,256,1]{3,2,4,1,0:T(8,128)S(1)} fusion(bf16[2,4,9,32,256]{4,3,2,1,0:T(8,128)(2,1)S(1)} %fusion.38, bf16[2,4,9,256,256]{4,3,2,1,0:T(8,128)(2,1)} %bitcast.463), kind=kOutput, calls=%fused_computation.216 | convolution fusion | flops 301989888 | bytes 10878976 | tf_op jit(solution)/shard_map/abkci,abkij->abcj/dot_general | solution.py:62
  320.4 3.7 scatter_fusion.2
  324.5 36.9 %psum.68 = f32[32]{0:T(128)S(1)} all-reduce(f32[32]{0:T(128)S(1)} %fusion.18), channel_id=1, replica_groups=mesh['row'=4,'blk'=8] {'row','blk'}, use_global_device_ids=true, to_apply=%region_14.15 | all-reduce | flops 32 | bytes 256 | tf_op jit(solution)/shard_map/psum | solution.py:85
  361.6 42.0 %psum.69 = f32[32]{0:T(128)S(1)} all-reduce(f32[32]{0:T(128)S(1)} %get-tuple-element.9), channel_id=1, replica_groups=mesh['row'=4,'blk'=8] {'row','blk'}, use_global_device_ids=true, to_apply=%region_16.17 | all-reduce | flops 32 | bytes 256 | tf_op jit(solution)/shard_map/psum | solution.py:43
  405.7 30.6 %all-gather.3 = bf16[256,64]{1,0:T(8,128)(2,1)S(1)} all-gather(bf16[32,64]{1,0:T(8,128)(2,1)S(1)} %fusion.15), channel_id=5, replica_groups=mesh['row'=4,'blk'=8] {'blk'}, dimensions={0}, use_global_device_ids=true | all-gather | bytes 36864 | tf_op jit(solution)/shard_map/all_gather | solution.py:70
  442.0 5.1 collective-permute-done.14
  447.3 5.4 %fusion.98 = f32[2,4,32,256,1]{3,2,4,1,0:T(8,128)S(1)} fusion(bf16[2,4,9,32,256]{4,3,2,1,0:T(8,128)(2,1)S(1)} %fusion.28, bf16[2,4,9,256,256]{4,3,2,1,0:T(8,128)(2,1)} %bitcast.464), kind=kOutput, calls=%fused_computation.217 | convolution fusion | flops 301989888 | bytes 10878976 | tf_op jit(solution)/shard_map/abkci,abkij->abcj/dot_general | solution.py:62
  453.3 3.7 scatter_fusion.3
  457.4 36.9 %psum.70 = f32[32]{0:T(128)S(1)} all-reduce(f32[32]{0:T(128)S(1)} %fusion.17), channel_id=1, replica_groups=mesh['row'=4,'blk'=8] {'row','blk'}, use_global_device_ids=true, to_apply=%region_19.20 | all-reduce | flops 32 | bytes 256 | tf_op jit(solution)/shard_map/psum | solution.py:85
  495.3 41.7 %psum.71 = f32[32]{0:T(128)S(1)} all-reduce(f32[32]{0:T(128)S(1)} %get-tuple-element.5), channel_id=1, replica_groups=mesh['row'=4,'blk'=8] {'row','blk'}, use_global_device_ids=true, to_apply=%region_21.22 | all-reduce | flops 32 | bytes 256 | tf_op jit(solution)/shard_map/psum | solution.py:92
  (153 shorter events, 41.6 us)
Async XLA Ops:
  0.6 5.0 copy-start
  0.6 4.0 copy-start.4
  0.7 36.0 %copy-start.5 = (s32[1,1,7]{2,1,0:T(1,128)S(1)}, s32[1,1,7]{2,1,0:T(1,128)}, u32[]{:S(2)}) copy-start(s32[1,1,7]{2,1,0:T(1,128)} %param.12) | copy-start | bytes 88
  0.7 40.9 %copy-start.2 = (bf16[1,1,7,64,64]{4,3,2,1,0:T(8,128)(2,1)S(1)}, bf16[1,1,7,64,64]{4,3,2,1,0:T(8,128)(2,1)}, u32[]{:S(2)}) copy-start(bf16[1,1,7,64,64]{4,3,2,1,0:T(8,128)(2,1)} %param.13) | copy-start | bytes 172036
  1.9 39.9 %copy-start.1 = (f32[1,1,8,32,256]{4,3,2,1,0:T(8,128)S(1)}, f32[1,1,8,32,256]{4,3,2,1,0:T(8,128)}, u32[]{:S(2)}) copy-start(f32[1,1,8,32,256]{4,3,2,1,0:T(8,128)} %param.7) | copy-start | bytes 786436
  1.9 35.3 %collective-permute-start.1 = (bf16[1,4,32,256]{3,2,1,0:T(8,128)(2,1)S(1)}, bf16[1,4,32,256]{3,2,1,0:T(8,128)(2,1)S(1)}, u32[]{:S(2)}, u32[]{:S(2)}) collective-permute-start(bf16[1,4,32,256]{3,2,1,0:T(8,128)(2,1)S(1)} %get-tuple-element.45), channel_id=1, source_target_pairs={{8,0},{16,8},{24,16},{0,24},{9,1},{17,9},{25,17},{1,25},{10,2},{18... | collective-permute-start | bytes 196616 | tf_op jit(solution)/shard_map/ppermute | solution.py:19
  4.4 32.9 %collective-permute-start = (bf16[1,4,32,256]{3,2,1,0:T(8,128)(2,1)S(1)}, bf16[1,4,32,256]{3,2,1,0:T(8,128)(2,1)S(1)}, u32[]{:S(2)}, u32[]{:S(2)}) collective-permute-start(bf16[1,4,32,256]{3,2,1,0:T(8,128)(2,1)S(1)} %get-tuple-element.44), channel_id=1, source_target_pairs={{0,8},{8,16},{16,24},{24,0},{1,9},{9,17},{17,25},{25,1},{2,10},{10... | collective-permute-start | bytes 196616 | tf_op jit(solution)/shard_map/ppermute | solution.py:18
  37.3 6.1 %collective-permute-start.3 = (bf16[4,1,32,256]{3,2,1,0:T(8,128)(2,1)S(1)}, bf16[4,1,32,256]{3,2,1,0:T(8,128)(2,1)S(1)}, u32[]{:S(2)}, u32[]{:S(2)}) collective-permute-start(bf16[4,1,32,256]{3,2,1,0:T(8,128)(2,1)S(1)} %get-tuple-element.36), channel_id=1, source_target_pairs={{1,0},{2,1},{3,2},{4,3},{5,4},{6,5},{7,6},{0,7},{9,8},{10,9},{11,1... | collective-permute-start | bytes 196616 | tf_op jit(solution)/shard_map/ppermute | solution.py:19
  41.5 7.0 %collective-permute-start.2 = (bf16[4,1,32,256]{3,2,1,0:T(8,128)(2,1)S(1)}, bf16[4,1,32,256]{3,2,1,0:T(8,128)(2,1)S(1)}, u32[]{:S(2)}, u32[]{:S(2)}) collective-permute-start(bf16[4,1,32,256]{3,2,1,0:T(8,128)(2,1)S(1)} %get-tuple-element.37), channel_id=1, source_target_pairs={{0,1},{1,2},{2,3},{3,4},{4,5},{5,6},{6,7},{7,0},{8,9},{9,10},{10,1... | collective-permute-start | bytes 196616 | tf_op jit(solution)/shard_map/ppermute | solution.py:18
  48.7 5.4 %copy-start.3 = (f32[1,1,8,256]{3,2,1,0:T(8,128)S(1)}, f32[1,1,8,256]{3,2,1,0:T(8,128)}, u32[]{:S(2)}) copy-start(f32[1,1,8,256]{3,2,1,0:T(8,128)} %param.8) | copy-start | bytes 24580
  138.2 33.1 %collective-permute-start.5 = (bf16[1,4,32,256]{3,2,1,0:T(8,128)(2,1)S(1)}, bf16[1,4,32,256]{3,2,1,0:T(8,128)(2,1)S(1)}, u32[]{:S(2)}, u32[]{:S(2)}) collective-permute-start(bf16[1,4,32,256]{3,2,1,0:T(8,128)(2,1)S(1)} %get-tuple-element.43), channel_id=1, source_target_pairs={{8,0},{16,8},{24,16},{0,24},{9,1},{17,9},{25,17},{1,25},{10,2},{18... | collective-permute-start | bytes 196616 | tf_op jit(solution)/shard_map/ppermute | solution.py:19
  138.6 32.7 %collective-permute-start.4 = (bf16[1,4,32,256]{3,2,1,0:T(8,128)(2,1)S(1)}, bf16[1,4,32,256]{3,2,1,0:T(8,128)(2,1)S(1)}, u32[]{:S(2)}, u32[]{:S(2)}) collective-permute-start(bf16[1,4,32,256]{3,2,1,0:T(8,128)(2,1)S(1)} %get-tuple-element.42), channel_id=1, source_target_pairs={{0,8},{8,16},{16,24},{24,0},{1,9},{9,17},{17,25},{25,1},{2,10},{10... | collective-permute-start | bytes 196616 | tf_op jit(solution)/shard_map/ppermute | solution.py:18
  171.4 5.2 collective-permute-start.7
  174.6 7.0 %collective-permute-start.6 = (bf16[4,1,32,256]{3,2,1,0:T(8,128)(2,1)S(1)}, bf16[4,1,32,256]{3,2,1,0:T(8,128)(2,1)S(1)}, u32[]{:S(2)}, u32[]{:S(2)}) collective-permute-start(bf16[4,1,32,256]{3,2,1,0:T(8,128)(2,1)S(1)} %get-tuple-element.31), channel_id=1, source_target_pairs={{0,1},{1,2},{2,3},{3,4},{4,5},{5,6},{6,7},{7,0},{8,9},{9,10},{10,1... | collective-permute-start | bytes 196616 | tf_op jit(solution)/shard_map/ppermute | solution.py:18
  270.8 33.2 %collective-permute-start.9 = (bf16[1,4,32,256]{3,2,1,0:T(8,128)(2,1)S(1)}, bf16[1,4,32,256]{3,2,1,0:T(8,128)(2,1)S(1)}, u32[]{:S(2)}, u32[]{:S(2)}) collective-permute-start(bf16[1,4,32,256]{3,2,1,0:T(8,128)(2,1)S(1)} %get-tuple-element.41), channel_id=1, source_target_pairs={{8,0},{16,8},{24,16},{0,24},{9,1},{17,9},{25,17},{1,25},{10,2},{18... | collective-permute-start | bytes 196616 | tf_op jit(solution)/shard_map/ppermute | solution.py:19
  271.5 32.5 %collective-permute-start.8 = (bf16[1,4,32,256]{3,2,1,0:T(8,128)(2,1)S(1)}, bf16[1,4,32,256]{3,2,1,0:T(8,128)(2,1)S(1)}, u32[]{:S(2)}, u32[]{:S(2)}) collective-permute-start(bf16[1,4,32,256]{3,2,1,0:T(8,128)(2,1)S(1)} %get-tuple-element.40), channel_id=1, source_target_pairs={{0,8},{8,16},{16,24},{24,0},{1,9},{9,17},{17,25},{25,1},{2,10},{10... | collective-permute-start | bytes 196616 | tf_op jit(solution)/shard_map/ppermute | solution.py:18
  304.1 5.1 collective-permute-start.11
  307.3 7.0 %collective-permute-start.10 = (bf16[4,1,32,256]{3,2,1,0:T(8,128)(2,1)S(1)}, bf16[4,1,32,256]{3,2,1,0:T(8,128)(2,1)S(1)}, u32[]{:S(2)}, u32[]{:S(2)}) collective-permute-start(bf16[4,1,32,256]{3,2,1,0:T(8,128)(2,1)S(1)} %get-tuple-element.27), channel_id=1, source_target_pairs={{0,1},{1,2},{2,3},{3,4},{4,5},{5,6},{6,7},{7,0},{8,9},{9,10},{10,1... | collective-permute-start | bytes 196616 | tf_op jit(solution)/shard_map/ppermute | solution.py:18
  403.7 33.1 %collective-permute-start.13 = (bf16[1,4,32,256]{3,2,1,0:T(8,128)(2,1)S(1)}, bf16[1,4,32,256]{3,2,1,0:T(8,128)(2,1)S(1)}, u32[]{:S(2)}, u32[]{:S(2)}) collective-permute-start(bf16[1,4,32,256]{3,2,1,0:T(8,128)(2,1)S(1)} %get-tuple-element.39), channel_id=1, source_target_pairs={{8,0},{16,8},{24,16},{0,24},{9,1},{17,9},{25,17},{1,25},{10,2},{18... | collective-permute-start | bytes 196616 | tf_op jit(solution)/shard_map/ppermute | solution.py:19
  404.1 32.8 %collective-permute-start.12 = (bf16[1,4,32,256]{3,2,1,0:T(8,128)(2,1)S(1)}, bf16[1,4,32,256]{3,2,1,0:T(8,128)(2,1)S(1)}, u32[]{:S(2)}, u32[]{:S(2)}) collective-permute-start(bf16[1,4,32,256]{3,2,1,0:T(8,128)(2,1)S(1)} %get-tuple-element.38), channel_id=1, source_target_pairs={{0,8},{8,16},{16,24},{24,0},{1,9},{9,17},{17,25},{25,1},{2,10},{10... | collective-permute-start | bytes 196616 | tf_op jit(solution)/shard_map/ppermute | solution.py:18
  436.9 5.1 collective-permute-start.15
  440.1 7.0 %collective-permute-start.14 = (bf16[4,1,32,256]{3,2,1,0:T(8,128)(2,1)S(1)}, bf16[4,1,32,256]{3,2,1,0:T(8,128)(2,1)S(1)}, u32[]{:S(2)}, u32[]{:S(2)}) collective-permute-start(bf16[4,1,32,256]{3,2,1,0:T(8,128)(2,1)S(1)} %get-tuple-element.23), channel_id=1, source_target_pairs={{0,1},{1,2},{2,3},{3,4},{4,5},{5,6},{6,7},{7,0},{8,9},{9,10},{10,1... | collective-permute-start | bytes 196616 | tf_op jit(solution)/shard_map/ppermute | solution.py:18
where the time goes:
time: 539 us; the launch traced here: 538 us
  blocking collectives  438 us (81%)
  waiting for transfers between devices  26.4 us (5%)
  matrix products  23.9 us (4%)
  other arithmetic  19.6 us (4%)
  starting transfers between devices  18.2 us (3%)
  local copies, waits for them, and re-layouts  10.6 us (2%)
    psum x4, blocking collectives, residual_sum(): return lax.psum(column_sum(values * values), ('row', 'blk'))  163 us
    all_gather x4, blocking collectives, local(): lax.all_gather(skeleton.astype(jnp.bfloat16)[None], 'blk', axis=0, tiled=...  123 us
    psum x3, blocking collectives, local(): curve = lax.psum(column_sum(direction * applied), ('row', 'blk'))  111 us
    psum x1, blocking collectives, local(): total = lax.psum(column_sum(right_side * solution), ('row', 'blk'))  41.7 us
    dot_general x4, matrix products, local(): jnp.einsum('abkci,abkij->abcj', sources, blocks_grid, preferred_element_t...  21.6 us
    ppermute x8, waiting for transfers between devices, extended_2(): before = lax.ppermute(last, axis, up)  20.2 us
    ppermute x8, starting transfers between devices, extended_2(): after = lax.ppermute(leading, axis, down)  17.8 us
    scatter-add x4, other arithmetic, local(): result = result.at[owner_leaf, :, owner_point].add(far_sum.T)  14.7 us
  transfers between devices with their start and end apart: 16, of which 8 were waited for; matrix products, arithmetic and copies ran while one was open for 2% of the time, Pallas kernels for 0%

commit v1 on v0

--- a/solution.py
+++ b/solution.py
@@ -2,6 +2,7 @@
 import jax.numpy as jnp
 from jax import lax
 from jax.sharding import PartitionSpec as P
+from jax.lax import psum
 
 ITERS = 4
 LEAF_ROWS = 2
@@ -82,7 +83,9 @@
         )
         result = result.at[owner_leaf, :, owner_point].add(far_sum.T)
         applied = (local_noise * direction[0, 0] + result)[None, None]
-        curve = lax.psum(column_sum(direction * applied), ("row", "blk"))
+        curve = column_sum(direction * applied)
+        for dd in ("blk", "row"):
+            curve = psum(curve, dd)
         step_size = norm_now / curve
         solution = solution + step_size[:, None] * direction
         residual = residual - step_size[:, None] * applied

time: 539 us -> 505 us (0.937)
  blocking collectives: 438 us -> 407 us
  waiting for transfers between devices: 26.4 us -> 20.1 us
    psum x3 -> x8, blocking collectives: 111 us -> 94.4 us  [local(): curve = psum(curve, dd)]
    psum x4, blocking collectives: 163 us -> 152 us  [residual_sum(): return lax.psum(column_sum(values * values), ('row', 'blk'))]
  transfers between devices with their start and end apart: 16 -> 16, of which waited for: 8 -> 6; matrix products, arithmetic and copies ran while one was open for 2% -> 2% of each run, Pallas kernels for 0% -> 0%
where the time goes in v1:
time: 505 us; the launch traced here: 503 us
  blocking collectives  407 us (81%)
  matrix products  23.9 us (5%)
  starting transfers between devices  20.3 us (4%)
  waiting for transfers between devices  20.1 us (4%)
  other arithmetic  19.6 us (4%)
  local copies, waits for them, and re-layouts  10.6 us (2%)
    psum x4, blocking collectives, residual_sum(): return lax.psum(column_sum(values * values), ('row', 'blk'))  152 us
    all_gather x4, blocking collectives, local(): lax.all_gather(skeleton.astype(jnp.bfloat16)[None], 'blk', axis=0, tiled=...  123 us
    psum x8, blocking collectives, local(): curve = psum(curve, dd)  94.4 us
    psum x1, blocking collectives, local(): total = lax.psum(column_sum(right_side * solution), ('row', 'blk'))  37.8 us
    dot_general x4, matrix products, local(): jnp.einsum('abkci,abkij->abcj', sources, blocks_grid, preferred_element_t...  21.6 us
    ppermute x8, starting transfers between devices, extended_2(): after = lax.ppermute(leading, axis, down)  20 us
    ppermute x8, waiting for transfers between devices, extended_2(): before = lax.ppermute(last, axis, up)  15.2 us
    scatter-add x4, other arithmetic, local(): result = result.at[owner_leaf, :, owner_point].add(far_sum.T)  14.7 us
  transfers between devices with their start and end apart: 16, of which 6 were waited for; matrix products, arithmetic and copies ran while one was open for 2% of the time, Pallas kernels for 0%

profile of v1, /device:TPU:0, one launch (start us, length us, event | category | flops | bytes accessed | tf_op | source)
XLA Modules:
  0.0 503.2 jit_solution(5280373268941284951)
XLA Ops:
  5.8 30.8 %all-gather = bf16[256,64]{1,0:T(8,128)(2,1)S(1)} all-gather(bf16[32,64]{1,0:T(8,128)(2,1)S(1)} %fusion.12), channel_id=2, replica_groups=mesh['row'=4,'blk'=8] {'blk'}, dimensions={0}, use_global_device_ids=true | all-gather | bytes 36864 | tf_op jit(solution)/shard_map/all_gather | solution.py:71
  41.7 39.6 %psum.91 = f32[32]{0:T(128)S(1)} all-reduce(f32[32]{0:T(128)S(1)} %get-tuple-element.30), channel_id=1, replica_groups=mesh['row'=4,'blk'=8] {'row','blk'}, use_global_device_ids=true, to_apply=%region_1.2 | all-reduce | flops 32 | bytes 256 | tf_op jit(solution)/shard_map/psum | solution.py:44
  82.1 5.4 %fusion.95 = f32[2,4,32,256,1]{3,2,4,1,0:T(8,128)S(1)} fusion(bf16[2,4,9,32,256]{4,3,2,1,0:T(8,128)(2,1)S(1)} %fusion.58, bf16[2,4,9,256,256]{4,3,2,1,0:T(8,128)(2,1)} %bitcast.461), kind=kOutput, calls=%fused_computation.214 | convolution fusion | flops 301989888 | bytes 10878976 | tf_op jit(solution)/shard_map/abkci,abkij->abcj/dot_general | solution.py:63
  92.3 20.4 %psum.92 = f32[32]{0:T(128)S(1)} all-reduce(f32[32]{0:T(128)S(1)} %fusion.16), channel_id=1, replica_groups=mesh['row'=4,'blk'=8] {'blk'}, use_global_device_ids=true, to_apply=%region_4.5 | all-reduce | flops 32 | bytes 256 | tf_op jit(solution)/shard_map/psum | solution.py:88
  112.7 5.6 %psum.93 = f32[32]{0:T(128)S(1)} all-reduce(f32[32]{0:T(128)S(1)} %psum.92), channel_id=1, replica_groups=mesh['row'=4,'blk'=8] {'row'}, use_global_device_ids=true, to_apply=%region_5.6 | all-reduce | flops 32 | bytes 256 | tf_op jit(solution)/shard_map/psum | solution.py:88
  118.6 36.9 %psum.94 = f32[32]{0:T(128)S(1)} all-reduce(f32[32]{0:T(128)S(1)} %multiply_reduce_fusion.3), channel_id=1, replica_groups=mesh['row'=4,'blk'=8] {'row','blk'}, use_global_device_ids=true, to_apply=%region_7.8 | all-reduce | flops 32 | bytes 256 | tf_op jit(solution)/shard_map/psum | solution.py:44
  157.6 30.5 %all-gather.1 = bf16[256,64]{1,0:T(8,128)(2,1)S(1)} all-gather(bf16[32,64]{1,0:T(8,128)(2,1)S(1)} %fusion.13), channel_id=3, replica_groups=mesh['row'=4,'blk'=8] {'blk'}, dimensions={0}, use_global_device_ids=true | all-gather | bytes 36864 | tf_op jit(solution)/shard_map/all_gather | solution.py:71
  194.6 5.1 %collective-permute-done.6 = bf16[4,1,32,256]{3,2,1,0:T(8,128)(2,1)S(1)} collective-permute-done((bf16[4,1,32,256]{3,2,1,0:T(8,128)(2,1)S(1)}, bf16[4,1,32,256]{3,2,1,0:T(8,128)(2,1)S(1)}, u32[]{:S(2)}, u32[]{:S(2)}) %collective-permute-start.6) | collective-permute-done | bytes 65568 | tf_op jit(solution)/shard_map/ppermute | solution.py:19
  199.9 5.4 %fusion.96 = f32[2,4,32,256,1]{3,2,4,1,0:T(8,128)S(1)} fusion(bf16[2,4,9,32,256]{4,3,2,1,0:T(8,128)(2,1)S(1)} %fusion.48, bf16[2,4,9,256,256]{4,3,2,1,0:T(8,128)(2,1)} %bitcast.462), kind=kOutput, calls=%fused_computation.215 | convolution fusion | flops 301989888 | bytes 10878976 | tf_op jit(solution)/shard_map/abkci,abkij->abcj/dot_general | solution.py:63
  210.0 17.1 %psum.95 = f32[32]{0:T(128)S(1)} all-reduce(f32[32]{0:T(128)S(1)} %fusion.19), channel_id=1, replica_groups=mesh['row'=4,'blk'=8] {'blk'}, use_global_device_ids=true, to_apply=%region_10.11 | all-reduce | flops 32 | bytes 256 | tf_op jit(solution)/shard_map/psum | solution.py:88
  227.1 5.6 %psum.96 = f32[32]{0:T(128)S(1)} all-reduce(f32[32]{0:T(128)S(1)} %psum.95), channel_id=1, replica_groups=mesh['row'=4,'blk'=8] {'row'}, use_global_device_ids=true, to_apply=%region_11.12 | all-reduce | flops 32 | bytes 256 | tf_op jit(solution)/shard_map/psum | solution.py:88
  233.0 37.8 %psum.97 = f32[32]{0:T(128)S(1)} all-reduce(f32[32]{0:T(128)S(1)} %get-tuple-element.11), channel_id=1, replica_groups=mesh['row'=4,'blk'=8] {'row','blk'}, use_global_device_ids=true, to_apply=%region_13.14 | all-reduce | flops 32 | bytes 256 | tf_op jit(solution)/shard_map/psum | solution.py:44
  273.0 30.7 %all-gather.2 = bf16[256,64]{1,0:T(8,128)(2,1)S(1)} all-gather(bf16[32,64]{1,0:T(8,128)(2,1)S(1)} %fusion.14), channel_id=4, replica_groups=mesh['row'=4,'blk'=8] {'blk'}, dimensions={0}, use_global_device_ids=true | all-gather | bytes 36864 | tf_op jit(solution)/shard_map/all_gather | solution.py:71
  310.2 5.1 %collective-permute-done.10 = bf16[4,1,32,256]{3,2,1,0:T(8,128)(2,1)S(1)} collective-permute-done((bf16[4,1,32,256]{3,2,1,0:T(8,128)(2,1)S(1)}, bf16[4,1,32,256]{3,2,1,0:T(8,128)(2,1)S(1)}, u32[]{:S(2)}, u32[]{:S(2)}) %collective-permute-start.10) | collective-permute-done | bytes 65568 | tf_op jit(solution)/shard_map/ppermute | solution.py:19
  315.5 5.4 %fusion.97 = f32[2,4,32,256,1]{3,2,4,1,0:T(8,128)S(1)} fusion(bf16[2,4,9,32,256]{4,3,2,1,0:T(8,128)(2,1)S(1)} %fusion.38, bf16[2,4,9,256,256]{4,3,2,1,0:T(8,128)(2,1)} %bitcast.463), kind=kOutput, calls=%fused_computation.216 | convolution fusion | flops 301989888 | bytes 10878976 | tf_op jit(solution)/shard_map/abkci,abkij->abcj/dot_general | solution.py:63
  325.5 17.1 %psum.98 = f32[32]{0:T(128)S(1)} all-reduce(f32[32]{0:T(128)S(1)} %fusion.18), channel_id=1, replica_groups=mesh['row'=4,'blk'=8] {'blk'}, use_global_device_ids=true, to_apply=%region_16.17 | all-reduce | flops 32 | bytes 256 | tf_op jit(solution)/shard_map/psum | solution.py:88
  342.6 5.6 %psum.99 = f32[32]{0:T(128)S(1)} all-reduce(f32[32]{0:T(128)S(1)} %psum.98), channel_id=1, replica_groups=mesh['row'=4,'blk'=8] {'row'}, use_global_device_ids=true, to_apply=%region_17.18 | all-reduce | flops 32 | bytes 256 | tf_op jit(solution)/shard_map/psum | solution.py:88
  348.5 38.0 %psum.100 = f32[32]{0:T(128)S(1)} all-reduce(f32[32]{0:T(128)S(1)} %get-tuple-element.7), channel_id=1, replica_groups=mesh['row'=4,'blk'=8] {'row','blk'}, use_global_device_ids=true, to_apply=%region_19.20 | all-reduce | flops 32 | bytes 256 | tf_op jit(solution)/shard_map/psum | solution.py:44
  388.6 30.5 %all-gather.3 = bf16[256,64]{1,0:T(8,128)(2,1)S(1)} all-gather(bf16[32,64]{1,0:T(8,128)(2,1)S(1)} %fusion.15), channel_id=5, replica_groups=mesh['row'=4,'blk'=8] {'blk'}, dimensions={0}, use_global_device_ids=true | all-gather | bytes 36864 | tf_op jit(solution)/shard_map/all_gather | solution.py:71
  425.7 5.1 %collective-permute-done.14 = bf16[4,1,32,256]{3,2,1,0:T(8,128)(2,1)S(1)} collective-permute-done((bf16[4,1,32,256]{3,2,1,0:T(8,128)(2,1)S(1)}, bf16[4,1,32,256]{3,2,1,0:T(8,128)(2,1)S(1)}, u32[]{:S(2)}, u32[]{:S(2)}) %collective-permute-start.14) | collective-permute-done | bytes 65568 | tf_op jit(solution)/shard_map/ppermute | solution.py:19
  430.9 5.4 %fusion.98 = f32[2,4,32,256,1]{3,2,4,1,0:T(8,128)S(1)} fusion(bf16[2,4,9,32,256]{4,3,2,1,0:T(8,128)(2,1)S(1)} %fusion.28, bf16[2,4,9,256,256]{4,3,2,1,0:T(8,128)(2,1)} %bitcast.464), kind=kOutput, calls=%fused_computation.217 | convolution fusion | flops 301989888 | bytes 10878976 | tf_op jit(solution)/shard_map/abkci,abkij->abcj/dot_general | solution.py:63
  441.0 17.1 %psum.101 = f32[32]{0:T(128)S(1)} all-reduce(f32[32]{0:T(128)S(1)} %fusion.17), channel_id=1, replica_groups=mesh['row'=4,'blk'=8] {'blk'}, use_global_device_ids=true, to_apply=%region_22.23 | all-reduce | flops 32 | bytes 256 | tf_op jit(solution)/shard_map/psum | solution.py:88
  458.1 5.6 %psum.102 = f32[32]{0:T(128)S(1)} all-reduce(f32[32]{0:T(128)S(1)} %psum.101), channel_id=1, replica_groups=mesh['row'=4,'blk'=8] {'row'}, use_global_device_ids=true, to_apply=%region_23.24 | all-reduce | flops 32 | bytes 256 | tf_op jit(solution)/shard_map/psum | solution.py:88
  464.8 37.8 %psum.103 = f32[32]{0:T(128)S(1)} all-reduce(f32[32]{0:T(128)S(1)} %get-tuple-element.3), channel_id=1, replica_groups=mesh['row'=4,'blk'=8] {'row','blk'}, use_global_device_ids=true, to_apply=%region_25.26 | all-reduce | flops 32 | bytes 256 | tf_op jit(solution)/shard_map/psum | solution.py:95
  (158 shorter events, 57.7 us)
Async XLA Ops:
  0.6 5.0 copy-start
  0.6 4.0 copy-start.4
  0.7 36.0 %copy-start.5 = (s32[1,1,7]{2,1,0:T(1,128)S(1)}, s32[1,1,7]{2,1,0:T(1,128)}, u32[]{:S(2)}) copy-start(s32[1,1,7]{2,1,0:T(1,128)} %param.12) | copy-start | bytes 88
  0.7 40.9 %copy-start.2 = (bf16[1,1,7,64,64]{4,3,2,1,0:T(8,128)(2,1)S(1)}, bf16[1,1,7,64,64]{4,3,2,1,0:T(8,128)(2,1)}, u32[]{:S(2)}) copy-start(bf16[1,1,7,64,64]{4,3,2,1,0:T(8,128)(2,1)} %param.13) | copy-start | bytes 172036
  1.9 79.5 %copy-start.1 = (f32[1,1,8,32,256]{4,3,2,1,0:T(8,128)S(1)}, f32[1,1,8,32,256]{4,3,2,1,0:T(8,128)}, u32[]{:S(2)}) copy-start(f32[1,1,8,32,256]{4,3,2,1,0:T(8,128)} %param.7) | copy-start | bytes 786436
  1.9 35.3 %collective-permute-start.1 = (bf16[1,4,32,256]{3,2,1,0:T(8,128)(2,1)S(1)}, bf16[1,4,32,256]{3,2,1,0:T(8,128)(2,1)S(1)}, u32[]{:S(2)}, u32[]{:S(2)}) collective-permute-start(bf16[1,4,32,256]{3,2,1,0:T(8,128)(2,1)S(1)} %get-tuple-element.43), channel_id=1, source_target_pairs={{8,0},{16,8},{24,16},{0,24},{9,1},{17,9},{25,17},{1,25},{10,2},{18... | collective-permute-start | bytes 196616 | tf_op jit(solution)/shard_map/ppermute | solution.py:20
  4.4 32.9 %collective-permute-start = (bf16[1,4,32,256]{3,2,1,0:T(8,128)(2,1)S(1)}, bf16[1,4,32,256]{3,2,1,0:T(8,128)(2,1)S(1)}, u32[]{:S(2)}, u32[]{:S(2)}) collective-permute-start(bf16[1,4,32,256]{3,2,1,0:T(8,128)(2,1)S(1)} %get-tuple-element.42), channel_id=1, source_target_pairs={{0,8},{8,16},{16,24},{24,0},{1,9},{9,17},{17,25},{25,1},{2,10},{10... | collective-permute-start | bytes 196616 | tf_op jit(solution)/shard_map/ppermute | solution.py:19
  37.3 44.5 %collective-permute-start.3 = (bf16[4,1,32,256]{3,2,1,0:T(8,128)(2,1)S(1)}, bf16[4,1,32,256]{3,2,1,0:T(8,128)(2,1)S(1)}, u32[]{:S(2)}, u32[]{:S(2)}) collective-permute-start(bf16[4,1,32,256]{3,2,1,0:T(8,128)(2,1)S(1)} %get-tuple-element.34), channel_id=1, source_target_pairs={{1,0},{2,1},{3,2},{4,3},{5,4},{6,5},{7,6},{0,7},{9,8},{10,9},{11,1... | collective-permute-start | bytes 196616 | tf_op jit(solution)/shard_map/ppermute | solution.py:20
  41.5 40.3 %collective-permute-start.2 = (bf16[4,1,32,256]{3,2,1,0:T(8,128)(2,1)S(1)}, bf16[4,1,32,256]{3,2,1,0:T(8,128)(2,1)S(1)}, u32[]{:S(2)}, u32[]{:S(2)}) collective-permute-start(bf16[4,1,32,256]{3,2,1,0:T(8,128)(2,1)S(1)} %get-tuple-element.35), channel_id=1, source_target_pairs={{0,1},{1,2},{2,3},{3,4},{4,5},{5,6},{6,7},{7,0},{8,9},{9,10},{10,1... | collective-permute-start | bytes 196616 | tf_op jit(solution)/shard_map/ppermute | solution.py:19
  82.1 5.4 %copy-start.3 = (f32[1,1,8,256]{3,2,1,0:T(8,128)S(1)}, f32[1,1,8,256]{3,2,1,0:T(8,128)}, u32[]{:S(2)}) copy-start(f32[1,1,8,256]{3,2,1,0:T(8,128)} %param.8) | copy-start | bytes 24580
  155.6 33.1 %collective-permute-start.5 = (bf16[1,4,32,256]{3,2,1,0:T(8,128)(2,1)S(1)}, bf16[1,4,32,256]{3,2,1,0:T(8,128)(2,1)S(1)}, u32[]{:S(2)}, u32[]{:S(2)}) collective-permute-start(bf16[1,4,32,256]{3,2,1,0:T(8,128)(2,1)S(1)} %get-tuple-element.41), channel_id=1, source_target_pairs={{8,0},{16,8},{24,16},{0,24},{9,1},{17,9},{25,17},{1,25},{10,2},{18... | collective-permute-start | bytes 196616 | tf_op jit(solution)/shard_map/ppermute | solution.py:20
  156.1 32.7 %collective-permute-start.4 = (bf16[1,4,32,256]{3,2,1,0:T(8,128)(2,1)S(1)}, bf16[1,4,32,256]{3,2,1,0:T(8,128)(2,1)S(1)}, u32[]{:S(2)}, u32[]{:S(2)}) collective-permute-start(bf16[1,4,32,256]{3,2,1,0:T(8,128)(2,1)S(1)} %get-tuple-element.40), channel_id=1, source_target_pairs={{0,8},{8,16},{16,24},{24,0},{1,9},{9,17},{17,25},{25,1},{2,10},{10... | collective-permute-start | bytes 196616 | tf_op jit(solution)/shard_map/ppermute | solution.py:19
  188.8 5.9 %collective-permute-start.7 = (bf16[4,1,32,256]{3,2,1,0:T(8,128)(2,1)S(1)}, bf16[4,1,32,256]{3,2,1,0:T(8,128)(2,1)S(1)}, u32[]{:S(2)}, u32[]{:S(2)}) collective-permute-start(bf16[4,1,32,256]{3,2,1,0:T(8,128)(2,1)S(1)} %get-tuple-element.28), channel_id=1, source_target_pairs={{1,0},{2,1},{3,2},{4,3},{5,4},{6,5},{7,6},{0,7},{9,8},{10,9},{11,1... | collective-permute-start | bytes 196616 | tf_op jit(solution)/shard_map/ppermute | solution.py:20
  192.7 7.0 %collective-permute-start.6 = (bf16[4,1,32,256]{3,2,1,0:T(8,128)(2,1)S(1)}, bf16[4,1,32,256]{3,2,1,0:T(8,128)(2,1)S(1)}, u32[]{:S(2)}, u32[]{:S(2)}) collective-permute-start(bf16[4,1,32,256]{3,2,1,0:T(8,128)(2,1)S(1)} %get-tuple-element.29), channel_id=1, source_target_pairs={{0,1},{1,2},{2,3},{3,4},{4,5},{5,6},{6,7},{7,0},{8,9},{9,10},{10,1... | collective-permute-start | bytes 196616 | tf_op jit(solution)/shard_map/ppermute | solution.py:19
  271.0 33.3 %collective-permute-start.9 = (bf16[1,4,32,256]{3,2,1,0:T(8,128)(2,1)S(1)}, bf16[1,4,32,256]{3,2,1,0:T(8,128)(2,1)S(1)}, u32[]{:S(2)}, u32[]{:S(2)}) collective-permute-start(bf16[1,4,32,256]{3,2,1,0:T(8,128)(2,1)S(1)} %get-tuple-element.39), channel_id=1, source_target_pairs={{8,0},{16,8},{24,16},{0,24},{9,1},{17,9},{25,17},{1,25},{10,2},{18... | collective-permute-start | bytes 196616 | tf_op jit(solution)/shard_map/ppermute | solution.py:20
  271.6 32.7 %collective-permute-start.8 = (bf16[1,4,32,256]{3,2,1,0:T(8,128)(2,1)S(1)}, bf16[1,4,32,256]{3,2,1,0:T(8,128)(2,1)S(1)}, u32[]{:S(2)}, u32[]{:S(2)}) collective-permute-start(bf16[1,4,32,256]{3,2,1,0:T(8,128)(2,1)S(1)} %get-tuple-element.38), channel_id=1, source_target_pairs={{0,8},{8,16},{16,24},{24,0},{1,9},{9,17},{17,25},{25,1},{2,10},{10... | collective-permute-start | bytes 196616 | tf_op jit(solution)/shard_map/ppermute | solution.py:19
  304.3 5.9 %collective-permute-start.11 = (bf16[4,1,32,256]{3,2,1,0:T(8,128)(2,1)S(1)}, bf16[4,1,32,256]{3,2,1,0:T(8,128)(2,1)S(1)}, u32[]{:S(2)}, u32[]{:S(2)}) collective-permute-start(bf16[4,1,32,256]{3,2,1,0:T(8,128)(2,1)S(1)} %get-tuple-element.24), channel_id=1, source_target_pairs={{1,0},{2,1},{3,2},{4,3},{5,4},{6,5},{7,6},{0,7},{9,8},{10,9},{11,1... | collective-permute-start | bytes 196616 | tf_op jit(solution)/shard_map/ppermute | solution.py:20
  308.3 7.0 %collective-permute-start.10 = (bf16[4,1,32,256]{3,2,1,0:T(8,128)(2,1)S(1)}, bf16[4,1,32,256]{3,2,1,0:T(8,128)(2,1)S(1)}, u32[]{:S(2)}, u32[]{:S(2)}) collective-permute-start(bf16[4,1,32,256]{3,2,1,0:T(8,128)(2,1)S(1)} %get-tuple-element.25), channel_id=1, source_target_pairs={{0,1},{1,2},{2,3},{3,4},{4,5},{5,6},{6,7},{7,0},{8,9},{9,10},{10,1... | collective-permute-start | bytes 196616 | tf_op jit(solution)/shard_map/ppermute | solution.py:19
  386.6 33.1 %collective-permute-start.13 = (bf16[1,4,32,256]{3,2,1,0:T(8,128)(2,1)S(1)}, bf16[1,4,32,256]{3,2,1,0:T(8,128)(2,1)S(1)}, u32[]{:S(2)}, u32[]{:S(2)}) collective-permute-start(bf16[1,4,32,256]{3,2,1,0:T(8,128)(2,1)S(1)} %get-tuple-element.37), channel_id=1, source_target_pairs={{8,0},{16,8},{24,16},{0,24},{9,1},{17,9},{25,17},{1,25},{10,2},{18... | collective-permute-start | bytes 196616 | tf_op jit(solution)/shard_map/ppermute | solution.py:20
  387.1 32.7 %collective-permute-start.12 = (bf16[1,4,32,256]{3,2,1,0:T(8,128)(2,1)S(1)}, bf16[1,4,32,256]{3,2,1,0:T(8,128)(2,1)S(1)}, u32[]{:S(2)}, u32[]{:S(2)}) collective-permute-start(bf16[1,4,32,256]{3,2,1,0:T(8,128)(2,1)S(1)} %get-tuple-element.36), channel_id=1, source_target_pairs={{0,8},{8,16},{16,24},{24,0},{1,9},{9,17},{17,25},{25,1},{2,10},{10... | collective-permute-start | bytes 196616 | tf_op jit(solution)/shard_map/ppermute | solution.py:19
  419.8 5.9 %collective-permute-start.15 = (bf16[4,1,32,256]{3,2,1,0:T(8,128)(2,1)S(1)}, bf16[4,1,32,256]{3,2,1,0:T(8,128)(2,1)S(1)}, u32[]{:S(2)}, u32[]{:S(2)}) collective-permute-start(bf16[4,1,32,256]{3,2,1,0:T(8,128)(2,1)S(1)} %get-tuple-element.20), channel_id=1, source_target_pairs={{1,0},{2,1},{3,2},{4,3},{5,4},{6,5},{7,6},{0,7},{9,8},{10,9},{11,1... | collective-permute-start | bytes 196616 | tf_op jit(solution)/shard_map/ppermute | solution.py:20
  423.7 7.0 %collective-permute-start.14 = (bf16[4,1,32,256]{3,2,1,0:T(8,128)(2,1)S(1)}, bf16[4,1,32,256]{3,2,1,0:T(8,128)(2,1)S(1)}, u32[]{:S(2)}, u32[]{:S(2)}) collective-permute-start(bf16[4,1,32,256]{3,2,1,0:T(8,128)(2,1)S(1)} %get-tuple-element.21), channel_id=1, source_target_pairs={{0,1},{1,2},{2,3},{3,4},{4,5},{5,6},{6,7},{7,0},{8,9},{9,10},{10,1... | collective-permute-start | bytes 196616 | tf_op jit(solution)/shard_map/ppermute | solution.py:19
